TPU v7x, 128 devices: a whole 4x4x4 slice. The times are simulated.
128 devices in a mesh: state: 4 (over z_hi, core), row: 32 (over z_lo, x, y).
Axes of the slice: x: 4, y: 4, z: 4 (z_hi: 2, z_lo: 2; z = z_hi * 2 + z_lo), core: 2. Of those that a mesh axis runs over, the one named last changes fastest.
Arguments:
- vectors: bfloat16 [131072, 512], P('row', 'state'), as said below
- active: int32 [8], replicated, may hold values 0 or 1
Outputs:
- orthonormal: bfloat16 [131072, 512], P('row', 'state')
Inputs may be any that keep to these rules, and one draw needn't show every extreme that they name: Each row and each column of vectors has its own scale.
All inputs are finite; a program needn't handle non-finite values.
Results may differ from a plain program's by a relative error of at most 0.00096.
Values may be sent and summed in bfloat16 or wider, within the bound.
A program may use at most 64 MiB of HBM per device.

v0:
```python
import jax
import jax.numpy as jnp
from jax import lax
from jax.sharding import PartitionSpec as P

VECS = 64
ITERS = 5


def newton_schulz(gram_matrix, total_rows):
    identity = jnp.eye(gram_matrix.shape[0], dtype=jnp.float32)
    frob_norm = jnp.sqrt(jnp.sum(gram_matrix * gram_matrix))
    current = gram_matrix / frob_norm
    inverse = identity
    for repeat in range(ITERS):
        newton_step = 0.5 * (
            3.0 * identity - jnp.dot(inverse, current, precision=lax.Precision.HIGHEST)
        )
        current = jnp.dot(current, newton_step, precision=lax.Precision.HIGHEST)
        inverse = jnp.dot(newton_step, inverse, precision=lax.Precision.HIGHEST)
    return (inverse * jnp.sqrt(total_rows / frob_norm)).astype(jnp.bfloat16)


def cross_product(left_block, right_block):
    return lax.dot_general(
        left_block, right_block, (((0,), (0,)), ((), ())), preferred_element_type=jnp.float32
    )


def shards(vectors, active):
    block_width = vectors.shape[1]
    total_rows = vectors.shape[0] * lax.axis_size("row")
    start_col = lax.axis_index("state") * block_width
    flag_all = jnp.repeat(active.astype(jnp.float32), VECS)
    flag_cols = lax.dynamic_slice_in_dim(flag_all, start_col, block_width, 0)
    masked = vectors * flag_cols.astype(jnp.bfloat16)
    gathered = lax.all_gather(masked, "state", axis=1, tiled=True)
    gram_matrix = cross_product(gathered, gathered)
    gram_matrix = lax.psum(gram_matrix, "row")
    gram_matrix = gram_matrix + jnp.diag((1.0 - flag_all) * total_rows)
    factor = newton_schulz(gram_matrix, total_rows)
    my_factor = lax.dynamic_slice_in_dim(factor, start_col, block_width, 1)
    result = jnp.dot(gathered, my_factor, preferred_element_type=jnp.float32)
    result = result + (1.0 - flag_cols) * vectors.astype(jnp.float32)
    return result.astype(jnp.bfloat16)


def solution(mesh):
    in_specs = (P("row", "state"), P())
    out_specs = P("row", "state")
    return jax.shard_map(shards, mesh=mesh, in_specs=in_specs, out_specs=out_specs, check_vma=False)
```

profile of v0, /device:TPU:0, one launch (start us, length us, event | category | flops | bytes accessed | tf_op | source)
XLA Modules:
  0.0 406.8 jit_solution(8900050890068867705)
XLA Ops:
  6.5 0.0 all-gather.2.cloned.1.call-start
  6.5 0.7 convert_element_type.16
  7.2 0.1 broadcast_in_dim.21
  7.3 0.1 reshape.11
  7.3 0.1 dynamic_slice.15
  7.4 2.3 broadcast_multiply_fusion
  9.7 0.0 all-gather.2.cloned.1.call-update
  9.7 0.0 all-reduce.2.cloned.1.call-start
  9.8 41.8 %all-gather.2.cloned.1.call-done = bf16[4096,512]{1,0:T(8,128)(2,1)} async-done(((bf16[4096,128]{1,0:T(8,128)(2,1)}), bf16[4096,512]{1,0:T(8,128)(2,1)}) %all-gather.2.cloned.1.call-update) | async-done | bytes 4194320 | tf_op jit(solution)/shard_map/all_gather | solution.py:37
  51.5 6.8 %fusion.15 = f32[512,512]{1,0:T(8,128)} fusion(bf16[4096,512]{1,0:T(8,128)(2,1)} %all-gather.2.cloned.1.call-done), kind=kOutput, calls=%fused_computation.26 | convolution fusion | flops 2147483648 | bytes 5242880 | tf_op jit(solution)/shard_map/dot_general | solution.py:25
  58.3 0.0 all-reduce.2.cloned.1.call-update
  58.4 0.1 broadcast_subtract_fusion
  58.4 310.3 %all-reduce.2.cloned.1.call-done = f32[512,512]{1,0:T(8,128)} async-done(((f32[512,512]{1,0:T(8,128)}), f32[512,512]{1,0:T(8,128)}) %all-reduce.2.cloned.1.call-update) | async-done | bytes 1048592 | tf_op jit(solution)/shard_map/psum | solution.py:39
  368.8 2.2 multiply_reduce_fusion
  371.6 0.0 copy-start.2
  371.7 2.4 fusion.5
  374.1 1.0 fusion.6
  375.1 0.0 copy-done.2
  375.1 1.9 fusion.12
  377.0 1.8 fusion.1
  378.8 1.8 fusion.17
  380.7 1.8 fusion.16
  382.6 2.0 fusion.2
  384.6 1.8 fusion.19
  386.5 1.8 fusion.18
  388.3 1.9 fusion.3
  390.2 1.8 fusion.20
  392.0 0.0 copy-start.1
  392.0 1.8 fusion.21
  394.0 0.0 copy-start
  394.0 1.9 fusion.4
  395.9 1.9 fusion.22
  397.7 0.0 copy-done.1
  397.7 0.0 copy-done
  397.7 2.2 fusion
  (1 shorter events, 0.0 us)
Async XLA Ops:
  6.5 45.0 %all-gather.2.cloned.1.call-start = ((), (), s32[]{:S(2)}) async-start(), calls=%async_computation | async-start | bytes 5242880 | tf_op jit(solution)/shard_map/all_gather | solution.py:37
  9.7 359.1 %all-reduce.2.cloned.1.call-start = ((), (), s32[]{:S(2)}) async-start(), calls=%async_computation.1 | async-start | bytes 2097152 | tf_op jit(solution)/shard_map/psum | solution.py:39
  371.6 3.4 copy-start.2
  392.0 5.7 %copy-start.1 = (bf16[4096,128]{1,0:T(8,128)(2,1)S(1)}, bf16[4096,128]{1,0:T(8,128)(2,1)}, u32[]{:S(2)}) copy-start(bf16[4096,128]{1,0:T(8,128)(2,1)} %param.2) | copy-start | bytes 3145732
  394.0 3.7 copy-start
Sparse Core Ops, SparseCore 0:
  9.8 41.6 all-gather.1
  58.5 310.2 all-reduce.1
where the time goes:
time: 407 us
  waiting for transfers between devices  352 us (86%)
  matrix products  34.9 us (9%)
  between operations  14.3 us (4%)
  other arithmetic  5.17 us (1%)
    psum x1, waiting for transfers between devices, shards(): gram_matrix = lax.psum(gram_matrix, 'row')  310 us
    all_gather x1, waiting for transfers between devices, shards(): gathered = lax.all_gather(masked, 'state', axis=1, tiled=True)  41.8 us
    dot_general x5, matrix products, newton_schulz(): jnp.dot(inverse, current, precision=lax.Precision.HIGHEST)  10 us
    dot_general x5, matrix products, newton_schulz(): inverse = jnp.dot(newton_step, inverse, precision=lax.Precision.HIGHEST)  8.37 us
  transfers between devices with their start and end apart: 2, of which 2 were waited for; matrix products, arithmetic and copies ran while one was open for 0% of the time, Pallas kernels for 0%

commit v1 on v0

v1 whole, which is shorter than its diff:
```python
import functools

import jax
import jax.numpy as jnp
from jax import lax
from jax.experimental import pallas as pl
from jax.experimental.pallas import tpu as pltpu
from jax.sharding import PartitionSpec as P

VECS = 64
MESH = pl.DeviceIdType.MESH
F32 = jnp.float32
BF16 = jnp.bfloat16
ANY = pl.BlockSpec(memory_space=pl.ANY)
VMEM = pl.BlockSpec(memory_space=pltpu.VMEM)

HALF, QUARTER, OWN, LINK, RELAY = 0, 1, 5, 6, 10
CORE, XDIM, YDIM, ZDIM, YBACK, XBACK, CBACK = 0, 1, 4, 7, 10, 13, 16
EARLY, LATE, SEMS = 14, 31, 48


def gram(left, right):
    return lax.dot_general(left, right, (((0,), (0,)), ((), ())), preferred_element_type=F32)


def exchange_kernel(
    vec_ref, early_ref, late_ref, rest_ref,
    half, quart, early_part, early_core, early_x, early_y, early_z, early_sum1, early_sum2, early_sum3,
    late_part, late_core, late_x, late_y, late_z, late_sum1, late_sum2, late_sum3,
    local_sem, send_sem, recv_sem,
):
    s, r = lax.axis_index("state"), lax.axis_index("row")
    zh, c = s // 2, s % 2
    zl, x, y = r // 16, (r // 4) % 4, r % 4
    z = zh * 2 + zl
    other_r = r + 16 * (1 - 2 * zl)
    partner = (s + 1 - 2 * c, r)
    rows = vec_ref.shape[0]
    half_rows, quart_rows = rows // 2, rows // 4

    def x_peer(d):
        return (s, zl * 16 + ((x + d) % 4) * 4 + y)

    def y_peer(d):
        return (s, zl * 16 + x * 4 + (y + d) % 4)

    def z_peer(d):
        to = (z + d) % 4
        return ((to // 2) * 2 + c, (to % 2) * 16 + x * 4 + y)

    def send(src, dst, sem, device, recv=None):
        return pltpu.make_async_remote_copy(
            src_ref=src, dst_ref=dst, send_sem=send_sem.at[sem],
            recv_sem=recv_sem.at[sem if recv is None else recv],
            device_id=device, device_id_type=MESH,
        )

    started = []

    def start(copies):
        for copy in copies:
            copy.start()
        started.extend(copies)
        return copies

    def arrive(copies):
        for copy in copies:
            copy.wait_recv()

    mine = pltpu.make_async_copy(vec_ref.at[pl.ds(c * half_rows, half_rows)], half.at[c], local_sem)
    mine.start()

    barrier = pltpu.get_barrier_semaphore()
    peers = [partner] + [(t, other_r) for t in range(4)] + [z_peer(2)]
    peers += [x_peer(d) for d in (1, 2, 3)] + [y_peer(d) for d in (1, 2, 3)]
    for peer in peers:
        pl.semaphore_signal(barrier, inc=1, device_id=peer, device_id_type=MESH)
    pl.semaphore_wait(barrier, len(peers))

    halves = start([send(vec_ref.at[pl.ds((1 - c) * half_rows, half_rows)], half.at[c], HALF, partner)])
    quarters = [
        send(vec_ref.at[pl.ds(t * quart_rows, quart_rows)], quart.at[s], QUARTER + t, (t, other_r), recv=QUARTER + s)
        for t in range(4)
    ]
    start(quarters)

    def quarters_arrive():
        for t in range(4):
            send(vec_ref.at[pl.ds(0, quart_rows)], quart.at[t], QUARTER + t, (t, other_r)).wait_recv()

    def core_step(part, got, base):
        return [send(part.at[pl.ds((1 - c) * 128, 128)], got, base + CORE, partner)]

    def x_step(sum1, got, base):
        return [
            send(sum1.at[pl.ds(((x + d) % 4) * 32, 32)], got.at[d - 1], base + XDIM + d - 1, x_peer(d)) for d in (1, 2, 3)
        ]

    def y_step(sum2, got, base):
        return [
            send(sum2.at[pl.ds(((y + d) % 4) * 8, 8)], got.at[d - 1], base + YDIM + d - 1, y_peer(d)) for d in (1, 2, 3)
        ]

    def z_step(sum3, got, base):
        return [send(sum3, got.at[z], base + ZDIM + d - 1, z_peer(d)) for d in (1, 2, 3)]

    def y_back(out, base):
        return [send(out.at[c, x, y], out.at[c, x, y], base + YBACK + d - 1, y_peer(d)) for d in (1, 2, 3)]

    def x_back(out, base):
        return [send(out.at[c, x], out.at[c, x], base + XBACK + d - 1, x_peer(d)) for d in (1, 2, 3)]

    def core_back(out, base):
        return [send(out.at[c], out.at[c], base + CBACK, partner)]

    mine.wait()
    arrive(halves)
    both = jnp.concatenate([half[0], half[1]], axis=1)
    early_part[...] = gram(both, both)
    step = start(core_step(early_part, early_core, EARLY))
    arrive(step)
    early_sum1[...] = early_part[pl.ds(pl.multiple_of(c * 128, 128), 128), :] + early_core[...]
    step = start(x_step(early_sum1, early_x, EARLY))
    start([send(vec_ref, rest_ref.at[0], OWN, partner)])
    arrive(step)
    early_sum2[...] = early_sum1[pl.ds(pl.multiple_of(x * 32, 32), 32), :] + early_x[0] + early_x[1] + early_x[2]
    step = start(y_step(early_sum2, early_y, EARLY))
    arrive(step)
    early_sum3[...] = early_sum2[pl.ds(pl.multiple_of(y * 8, 8), 8), :] + early_y[0] + early_y[1] + early_y[2]
    early_z[z] = early_sum3[...]

    quarters_arrive()
    early_step = start(z_step(early_sum3, early_z, EARLY))
    left = jnp.concatenate([quart[0], quart[1]], axis=1)
    right = jnp.concatenate([quart[2], quart[3]], axis=1)
    late_part[...] = gram(left, right)
    step = start(core_step(late_part, late_core, LATE))

    def link(part):
        return [
            send(
                quart.at[2 - 2 * to + part],
                rest_ref.at[1 + part, pl.ds(s * quart_rows, quart_rows)],
                LINK + part * 2 + to,
                (to * 2 + c, other_r),
                recv=LINK + part * 2 + zh,
            )
            for to in (0, 1)
        ]

    def link_arrive(part):
        for frm in (0, 1):
            send(
                quart.at[0], rest_ref.at[1 + part, pl.ds((frm * 2 + c) * quart_rows, quart_rows)],
                LINK + part * 2 + frm, partner,
            ).wait_recv()

    def relay(part):
        blocks = [rest_ref.at[1 + part, pl.ds((frm * 2 + c) * quart_rows, quart_rows)] for frm in (0, 1)]
        return [send(block, block, RELAY + part * 2 + frm, partner) for frm, block in enumerate(blocks)]

    def relay_arrive(part):
        blocks = [rest_ref.at[1 + part, pl.ds((frm * 2 + 1 - c) * quart_rows, quart_rows)] for frm in (0, 1)]
        for frm, block in enumerate(blocks):
            send(block, block, RELAY + part * 2 + frm, partner).wait_recv()

    start(link(0))
    arrive(step)
    late_sum1[...] = late_part[pl.ds(pl.multiple_of(c * 128, 128), 128), :] + late_core[...]
    step = start(x_step(late_sum1, late_x, LATE))
    arrive(early_step)
    early_ref[c, x, y, 0] = early_z[0] + early_z[1]
    early_ref[c, x, y, 1] = early_z[2] + early_z[3]
    early_step = start(y_back(early_ref, EARLY))
    arrive(step)
    late_sum2[...] = late_sum1[pl.ds(pl.multiple_of(x * 32, 32), 32), :] + late_x[0] + late_x[1] + late_x[2]
    step = start(y_step(late_sum2, late_y, LATE))
    arrive(early_step)
    early_step = start(x_back(early_ref, EARLY))
    arrive(step)
    late_sum3[...] = late_sum2[pl.ds(pl.multiple_of(y * 8, 8), 8), :] + late_y[0] + late_y[1] + late_y[2]
    late_z[z] = late_sum3[...]
    step = start(z_step(late_sum3, late_z, LATE))
    start(link(1))
    link_arrive(0)
    start(relay(0))
    arrive(step)
    late_ref[c, x, y] = late_z[0] + late_z[1] + late_z[2] + late_z[3]
    step = start(y_back(late_ref, LATE))
    arrive(early_step)
    early_step = start(core_back(early_ref, EARLY))
    arrive(step)
    step = start(x_back(late_ref, LATE))
    arrive(early_step)
    relay_arrive(0)
    arrive(step)
    step = start(core_back(late_ref, LATE))
    link_arrive(1)
    start(relay(1))
    arrive(step)
    relay_arrive(1)
    send(vec_ref, rest_ref.at[0], OWN, partner).wait_recv()
    for copy in started:
        copy.wait_send()


def exchange(vectors):
    rows, width = vectors.shape
    early = jax.ShapeDtypeStruct((2, 4, 4, 2, 8, 256), F32)
    late = jax.ShapeDtypeStruct((2, 4, 4, 8, 256), F32)
    rest = jax.ShapeDtypeStruct((3, rows, width), BF16)
    sums = [
        pltpu.VMEM((256, 256), F32), pltpu.VMEM((128, 256), F32), pltpu.VMEM((3, 32, 256), F32),
        pltpu.VMEM((3, 8, 256), F32), pltpu.VMEM((4, 8, 256), F32),
        pltpu.VMEM((128, 256), F32), pltpu.VMEM((32, 256), F32), pltpu.VMEM((8, 256), F32),
    ]
    return pl.pallas_call(
        exchange_kernel,
        out_shape=(early, late, rest),
        in_specs=[ANY],
        out_specs=(VMEM, VMEM, ANY),
        scratch_shapes=[
            pltpu.VMEM((2, rows // 2, width), BF16), pltpu.VMEM((4, rows // 4, width), BF16),
            *sums, *sums,
            pltpu.SemaphoreType.DMA, pltpu.SemaphoreType.DMA((SEMS,)), pltpu.SemaphoreType.DMA((SEMS,)),
        ],
        compiler_params=pltpu.CompilerParams(
            collective_id=0, has_side_effects=True, vmem_limit_bytes=24 * 2**20
        ),
        name="exchange",
    )(vectors)


def split(value):
    high = value.astype(BF16)
    return high, (value - high.astype(F32)).astype(BF16)


def product(left, right):
    (lh, ll), (rh, rl) = left, right
    dot = functools.partial(jnp.dot, preferred_element_type=F32)
    return dot(lh, rh) + (dot(lh, rl) + dot(ll, rh))


def finish_kernel(
    total_rows, active_ref, early_ref, late_ref, vec_ref, rest_ref, out_ref,
    matrix, factor, own, rest, result, in_sem, out_sem,
):
    s = lax.axis_index("state")
    zh, c = s // 2, s % 2
    rows = own.shape[0]
    loads = [pltpu.make_async_copy(vec_ref, own, in_sem.at[0])]
    loads += [pltpu.make_async_copy(rest_ref.at[k], rest.at[k], in_sem.at[1 + k]) for k in range(3)]
    for load in loads:
        load.start()

    def flags(shape, axis):
        state = lax.broadcasted_iota(jnp.int32, shape, axis) // VECS
        flag = jnp.zeros(shape, jnp.int32)
        for k in range(8):
            flag = jnp.where(state == k, active_ref[k], flag)
        return flag

    cols = matrix.shape[0]
    cross = late_ref[...].reshape(256, 256)
    matrix[0:256, 0:256] = early_ref[:, :, :, 0].reshape(256, 256)
    matrix[256:512, 256:512] = early_ref[:, :, :, 1].reshape(256, 256)
    matrix[0:256, 256:512] = cross
    matrix[256:512, 0:256] = cross.T
    row_flag, col_flag = flags((cols, 1), 0), flags((1, cols), 1)
    eye = lax.broadcasted_iota(jnp.int32, (cols, cols), 0) == lax.broadcasted_iota(jnp.int32, (cols, cols), 1)
    gram_matrix = jnp.where(row_flag * col_flag == 1, matrix[...], 0.0)
    gram_matrix = gram_matrix + jnp.where(eye & (row_flag == 0), total_rows, 0.0)
    frob_norm = jnp.sqrt(jnp.sum(gram_matrix * gram_matrix, keepdims=True))
    current = gram_matrix / frob_norm

    panel_eye = lax.broadcasted_iota(jnp.int32, (cols, 128), 0) == lax.broadcasted_iota(jnp.int32, (cols, 128), 1) + s * 128

    def advance(parts, current):
        first = 1.5 * current - 0.5 * product(parts, parts)
        return 1.5 * first - 0.5 * product(split(first), parts)

    matrix[...] = current
    column = matrix[:, pl.ds(pl.multiple_of(s * 128, 128), 128)]
    panel = jnp.where(panel_eye, 1.5, 0.0) - 0.5 * column
    parts = split(current)
    for step in range(2):
        current = advance(parts, current)
        parts = split(current)
        panel = 1.5 * panel - 0.5 * product(parts, split(panel))
    current = advance(parts, current)
    parts = split(current)
    moved = product(parts, split(panel))
    panel = 1.5 * panel - 0.5 * moved
    last = product(parts, split(panel))
    last = 1.5 * last - 0.5 * product(parts, split(last))
    last = 1.5 * last - 0.5 * product(parts, split(last))
    panel = 1.5 * panel - 0.5 * last
    panel = (panel * jnp.sqrt(total_rows / frob_norm)).astype(BF16)
    factor[...] = jnp.where(row_flag == 1, panel.astype(F32), 0.0)

    def factor_of(state):
        return factor[pl.ds(pl.multiple_of(state * 128, 128), 128), :].astype(BF16)

    near = jnp.concatenate([factor_of(s), factor_of(s + 1 - 2 * c)], axis=0)
    far = jnp.concatenate([factor_of(2 - 2 * zh), factor_of(3 - 2 * zh)], axis=0)
    keep = jnp.zeros((1, 128), jnp.int32)
    lane_state = lax.broadcasted_iota(jnp.int32, (1, 128), 1) // VECS + s * 2
    for k in range(8):
        keep = jnp.where(lane_state == k, active_ref[k], keep)
    for load in loads:
        load.wait()
    chunk = 512
    for k in range(rows // chunk):
        block = pl.ds(k * chunk, chunk)
        left = jnp.concatenate([own[block], rest[0, block]], axis=1)
        right = jnp.concatenate([rest[1, block], rest[2, block]], axis=1)
        value = jnp.dot(left, near, preferred_element_type=F32) + jnp.dot(right, far, preferred_element_type=F32)
        result[block] = jnp.where(keep == 1, value, own[block].astype(F32)).astype(BF16)
        pltpu.make_async_copy(result.at[block], out_ref.at[block], out_sem.at[k]).start()
    for k in range(rows // chunk):
        block = pl.ds(k * chunk, chunk)
        pltpu.make_async_copy(result.at[block], out_ref.at[block], out_sem.at[k]).wait()


def finish(total_rows, active, early, late, vectors, rest):
    rows, width = vectors.shape
    return pl.pallas_call(
        functools.partial(finish_kernel, total_rows),
        out_shape=jax.ShapeDtypeStruct((rows, width), BF16),
        in_specs=[pl.BlockSpec(memory_space=pltpu.SMEM), VMEM, VMEM, ANY, ANY],
        out_specs=ANY,
        scratch_shapes=[
            pltpu.VMEM((512, 512), F32), pltpu.VMEM((512, 128), F32),
            pltpu.VMEM((rows, width), BF16), pltpu.VMEM((3, rows, width), BF16), pltpu.VMEM((rows, width), BF16),
            pltpu.SemaphoreType.DMA((4,)), pltpu.SemaphoreType.DMA((8,)),
        ],
        compiler_params=pltpu.CompilerParams(vmem_limit_bytes=40 * 2**20),
        name="finish",
    )(active, early, late, vectors, rest)


def shards(vectors, active):
    total_rows = float(vectors.shape[0] * lax.axis_size("row"))
    early, late, rest = exchange(vectors)
    return finish(total_rows, active, early, late, vectors, rest)


def solution(mesh):
    in_specs = (P("row", "state"), P())
    out_specs = P("row", "state")
    return jax.shard_map(shards, mesh=mesh, in_specs=in_specs, out_specs=out_specs, check_vma=False)
```

time: 407 us -> 60.6 us (0.15)
  the two profiles are of different devices: /device:TPU:0 before, /device:TPU:1 now
where the time goes in v1:
time: 60.6 us; the launch traced here: 60.5 us
  Pallas kernels  57.3 us (95%)
  local copies, waits for them, and re-layouts  3.1 us (5%)
    pallas_call x1, Pallas kernels, exchange(): pl.pallas_call(exchange_kernel, out_shape=(early, late, rest), in_specs=[...  43.4 us
    pallas_call x1, Pallas kernels, finish(): pl.pallas_call(functools.partial(finish_kernel, total_rows), out_shape=ja...  14 us
    unnamed x6, local copies, waits for them, and re-layouts  3.1 us

profile of v1, /device:TPU:1, one launch (start us, length us, event | category | flops | bytes accessed | tf_op | source)
XLA Modules:
  0.0 60.5 jit_solution(9479971186843792941)
XLA Ops:
  0.0 0.0 copy-start
  0.0 1.2 %copy-done = bf16[4096,128]{1,0:T(8,128)(2,1)S(1)} copy-done((bf16[4096,128]{1,0:T(8,128)(2,1)S(1)}, bf16[4096,128]{1,0:T(8,128)(2,1)}, u32[]{:S(2)}) %copy-start) | copy-done | bytes 1048600
  1.2 43.4 %exchange.1 = (f32[2,4,4,2,8,256]{5,4,3,2,1,0:T(8,128)S(1)}, f32[2,4,4,8,256]{4,3,2,1,0:T(8,128)S(1)}, bf16[3,4096,128]{2,1,0:T(8,128)(2,1)S(1)}) custom-call(bf16[4096,128]{1,0:T(8,128)(2,1)S(1)} %copy-done), custom_call_target="tpu_custom_call" | custom-call | tf_op jit(solution)/shard_map/exchange/pallas_call | solution.py:217
  44.6 0.0 copy-start.1
  44.6 1.2 %copy-done.1 = bf16[4096,128]{1,0:T(8,128)(2,1)S(1)} copy-done((bf16[4096,128]{1,0:T(8,128)(2,1)S(1)}, bf16[4096,128]{1,0:T(8,128)(2,1)}, u32[]{:S(2)}) %copy-start.1) | copy-done | bytes 1048600
  45.8 0.0 copy-start.2
  45.8 0.7 %copy-done.2 = s32[8]{0:T(128)S(1)} copy-done((s32[8]{0:T(128)S(1)}, s32[8]{0:T(128)}, u32[]{:S(2)}) %copy-start.2) | copy-done | bytes 56
  46.5 14.0 %finish.1 = bf16[4096,128]{1,0:T(8,128)(2,1)} custom-call(s32[8]{0:T(128)S(1)} %copy-done.2, f32[2,4,4,2,8,256]{5,4,3,2,1,0:T(8,128)S(1)} %get-tuple-element.8.early_ref, f32[2,4,4,8,256]{4,3,2,1,0:T(8,128)S(1)} %get-tuple-element.9.late_ref, bf16[4096,128]{1,0:T(8,128)(2,1)S(1)} %copy-done.1, bf16[3,4096,128]{2,1,0:T(8,128)(2,1)S(1)} %get-tuple-element.10.rest_ref), custom_call_target="tpu_custom_call" | custom-call | tf_op jit(solution)/shard_map/finish/pallas_call | solution.py:328
Async XLA Ops:
  0.0 1.2 %copy-start = (bf16[4096,128]{1,0:T(8,128)(2,1)S(1)}, bf16[4096,128]{1,0:T(8,128)(2,1)}, u32[]{:S(2)}) copy-start(bf16[4096,128]{1,0:T(8,128)(2,1)} %vec_ref.3) | copy-start | bytes 3145732
  44.6 1.2 %copy-start.1 = (bf16[4096,128]{1,0:T(8,128)(2,1)S(1)}, bf16[4096,128]{1,0:T(8,128)(2,1)}, u32[]{:S(2)}) copy-start(bf16[4096,128]{1,0:T(8,128)(2,1)} %vec_ref.3) | copy-start | bytes 3145732
  45.8 0.7 %copy-start.2 = (s32[8]{0:T(128)S(1)}, s32[8]{0:T(128)}, u32[]{:S(2)}) copy-start(s32[8]{0:T(128)} %active_ref.1) | copy-start | bytes 100

commit v2 on v1

v2 whole, which is shorter than its diff:
```python
import functools

import jax
import jax.numpy as jnp
from jax import lax
from jax.experimental import pallas as pl
from jax.experimental.pallas import tpu as pltpu
from jax.sharding import PartitionSpec as P

VECS = 64
MESH = pl.DeviceIdType.MESH
F32 = jnp.float32
BF16 = jnp.bfloat16
ANY = pl.BlockSpec(memory_space=pl.ANY)
VMEM = pl.BlockSpec(memory_space=pltpu.VMEM)

HALF, QUARTER, OWN, LINK, RELAY, CORE, XDIM, YDIM, ZDIM, YBACK, XBACK, CBACK = 0, 1, 5, 6, 10, 14, 15, 18, 21, 24, 27, 30
LCORE, LOUT, LBACK, LCBACK, SEMS = 31, 32, 33, 34, 35
OFFSETS = [(a, b, d) for a in range(4) for b in range(4) for d in range(4)]


def hops(offset):
    return sum(min(v, 4 - v) for v in offset)


def gram(left, right):
    return lax.dot_general(left, right, (((0,), (0,)), ((), ())), preferred_element_type=F32)


def exchange_kernel(
    vec_ref, active_hbm, early_ref, late_ref, all_ref, flag_ref,
    active, half, quart, early_part, early_core, early_x, early_y, early_z, early_sum1, early_sum2, early_sum3,
    late_part, late_core, late_sum, late_got, mask, local_sem, send_sem, recv_sem,
):
    s, r = lax.axis_index("state"), lax.axis_index("row")
    zh, c = s // 2, s % 2
    zl, x, y = r // 16, (r // 4) % 4, r % 4
    z = zh * 2 + zl
    other_r = r + 16 * (1 - 2 * zl)
    near = s + 1 - 2 * c
    partner = (near, r)
    far = 2 - 2 * zh
    rows = vec_ref.shape[0]
    half_rows, quart_rows = rows // 2, rows // 4

    def device(offset):
        to_x, to_y, to_z = [(at + step) % 4 for at, step in zip((x, y, z), offset)]
        return ((to_z // 2) * 2 + c, (to_z % 2) * 16 + to_x * 4 + to_y)

    def x_peer(d):
        return device((d, 0, 0))

    def y_peer(d):
        return device((0, d, 0))

    def z_peer(d):
        return device((0, 0, d))

    def send(src, dst, sem, to, recv=None):
        return pltpu.make_async_remote_copy(
            src_ref=src, dst_ref=dst, send_sem=send_sem.at[sem],
            recv_sem=recv_sem.at[sem if recv is None else recv],
            device_id=to, device_id_type=MESH,
        )

    started = []

    def start(copies):
        for copy in copies:
            copy.start()
        started.extend(copies)
        return copies

    def arrive(copies):
        for copy in copies:
            copy.wait_recv()

    mine = pltpu.make_async_copy(vec_ref.at[pl.ds(c * half_rows, half_rows)], half.at[c], local_sem.at[0])
    mine.start()
    flag_copy = pltpu.make_async_copy(active_hbm, active, local_sem.at[1])
    flag_copy.start()
    own = pltpu.make_async_copy(vec_ref, all_ref.at[s], local_sem.at[2])
    own.start()

    barrier = pltpu.get_barrier_semaphore()
    peers = [partner] + [(t, other_r) for t in range(4)] + [z_peer(2)]
    peers += [x_peer(d) for d in (1, 2, 3)] + [y_peer(d) for d in (1, 2, 3)]
    for peer in peers:
        pl.semaphore_signal(barrier, inc=1, device_id=peer, device_id_type=MESH)
    pl.semaphore_wait(barrier, len(peers))

    halves = start([send(vec_ref.at[pl.ds((1 - c) * half_rows, half_rows)], half.at[c], HALF, partner)])
    start([
        send(vec_ref.at[pl.ds(t * quart_rows, quart_rows)], quart.at[s], QUARTER + t, (t, other_r), recv=QUARTER + s)
        for t in range(4)
    ])

    flag_copy.wait()

    def flags(shape, axis, first):
        state = lax.broadcasted_iota(jnp.int32, shape, axis) // VECS + first
        flag = jnp.zeros(shape, F32)
        for k in range(8):
            flag = jnp.where(state == k, active[k].astype(F32), flag)
        return flag

    flag_ref[...] = flags(flag_ref.shape, 1, 0)
    block = (256, 256)
    mask[...] = flags(block, 0, 0) * flags(block, 1, 4)
    early_mask = flags(block, 0, zh * 4) * flags(block, 1, zh * 4)

    mine.wait()
    arrive(halves)
    both = jnp.concatenate([half[0], half[1]], axis=1)
    early_part[...] = jnp.where(early_mask == 1.0, gram(both, both), 0.0)
    step = start([send(early_part.at[pl.ds((1 - c) * 128, 128)], early_core, CORE, partner)])
    arrive(step)
    early_sum1[...] = early_part[pl.ds(pl.multiple_of(c * 128, 128), 128), :] + early_core[...]
    step = start([
        send(early_sum1.at[pl.ds(((x + d) % 4) * 32, 32)], early_x.at[d - 1], XDIM + d - 1, x_peer(d)) for d in (1, 2, 3)
    ])
    start([send(vec_ref, all_ref.at[s], OWN, partner)])
    arrive(step)
    early_sum2[...] = early_sum1[pl.ds(pl.multiple_of(x * 32, 32), 32), :] + early_x[0] + early_x[1] + early_x[2]
    step = start([
        send(early_sum2.at[pl.ds(((y + d) % 4) * 8, 8)], early_y.at[d - 1], YDIM + d - 1, y_peer(d)) for d in (1, 2, 3)
    ])
    arrive(step)
    early_sum3[...] = early_sum2[pl.ds(pl.multiple_of(y * 8, 8), 8), :] + early_y[0] + early_y[1] + early_y[2]
    early_z[z] = early_sum3[...]
    early_step = start([send(early_sum3, early_z.at[z], ZDIM + d - 1, z_peer(d)) for d in (1, 2, 3)])

    for t in range(4):
        send(vec_ref.at[pl.ds(0, quart_rows)], quart.at[t], QUARTER + t, (t, other_r)).wait_recv()
    left = jnp.concatenate([quart[0], quart[1]], axis=1)
    right = jnp.concatenate([quart[2], quart[3]], axis=1)
    late_part[...] = jnp.where(mask[...] == 1.0, gram(left, right), 0.0)
    step = start([send(late_part.at[pl.ds((1 - c) * 128, 128)], late_core, LCORE, partner)])

    def link(part):
        return [
            send(
                quart.at[2 - 2 * to + part],
                all_ref.at[2 - 2 * to + part, pl.ds(s * quart_rows, quart_rows)],
                LINK + part * 2 + to,
                (to * 2 + c, other_r),
                recv=LINK + part * 2 + zh,
            )
            for to in (0, 1)
        ]

    def relay_copies(part, core):
        blocks = [all_ref.at[far + part, pl.ds((frm * 2 + core) * quart_rows, quart_rows)] for frm in (0, 1)]
        return [send(block, block, RELAY + part * 2 + frm, partner) for frm, block in enumerate(blocks)]

    def link_arrive(part):
        for frm in (0, 1):
            send(
                quart.at[0], all_ref.at[far + part, pl.ds((frm * 2 + c) * quart_rows, quart_rows)],
                LINK + part * 2 + frm, partner,
            ).wait_recv()

    arrive(step)
    total = late_part[pl.ds(pl.multiple_of(c * 128, 128), 128), :] + late_core[...]
    for k in (0, 1):
        late_sum[:, k] = total[:, k * 128:(k + 1) * 128].reshape(16, 8, 128)
    odd = (x + y + z + c) % 2
    place = x * 16 + y * 4 + z
    outward = sorted([(a, b, d) for a in range(4) for b in range(4) for d in (0, 2)], key=hops, reverse=True)

    def scatter(offset):
        a, b, d = offset
        d = d + (a + b + odd) % 2
        to_x, to_y, to_z = (x + a) % 4, (y + b) % 4, (z + d) % 4
        send(
            late_sum.at[to_x * 4 + to_y, to_z // 2], late_got.at[place], LOUT, device((a, b, d))
        ).start()

    for offset in outward:
        if offset == (0, 0, 0):
            pl.when(odd == 1)(functools.partial(scatter, offset))
        else:
            scatter(offset)
    start(link(0))
    arrive(early_step)
    early_ref[c, x, y, 0] = early_z[0] + early_z[1]
    early_ref[c, x, y, 1] = early_z[2] + early_z[3]
    early_step = start([
        send(early_ref.at[c, x, y], early_ref.at[c, x, y], YBACK + d - 1, y_peer(d)) for d in (1, 2, 3)
    ])
    arrive(early_step)

    here = (c, x * 4 + y, z // 2)

    @pl.when(odd == 0)
    def _():
        late_got[place] = late_sum[x * 4 + y, z // 2]
        whole = late_got.at[pl.ds(0, 63)]
        send(whole, whole, LOUT, partner).wait_recv()
        late_ref[here] = jnp.sum(late_got[...], axis=0)
        for offset in sorted(OFFSETS[1:], key=hops, reverse=True):
            send(late_ref.at[here], late_ref.at[here], LBACK, device(offset)).start()

    early_step = start([send(early_ref.at[c, x], early_ref.at[c, x], XBACK + d - 1, x_peer(d)) for d in (1, 2, 3)])
    start(link(1))
    link_arrive(0)
    start(relay_copies(0, c))
    arrive(early_step)
    early_step = start([send(early_ref.at[c], early_ref.at[c], CBACK, partner)])

    @pl.when(odd == 0)
    def _():
        gathered = late_got.at[pl.ds(0, 31)]
        send(gathered, gathered, LBACK, partner).wait_recv()

    @pl.when(odd == 1)
    def _():
        gathered = late_got.at[pl.ds(0, 32)]
        send(gathered, gathered, LBACK, partner).wait_recv()

    step = start([send(late_ref.at[c], late_ref.at[c], LCBACK, partner)])
    link_arrive(1)
    start(relay_copies(1, c))
    arrive(early_step)
    arrive(step)
    arrive(relay_copies(0, 1 - c))
    arrive(relay_copies(1, 1 - c))
    send(vec_ref, all_ref.at[near], OWN, partner).wait_recv()
    own.wait()

    @pl.when(odd == 0)
    def _():
        out, back = late_got.at[pl.ds(0, 31)], late_got.at[pl.ds(0, 63)]
        send(out, out, LOUT, partner).wait_send()
        send(back, back, LBACK, partner).wait_send()

    @pl.when(odd == 1)
    def _():
        out = late_got.at[pl.ds(0, 32)]
        send(out, out, LOUT, partner).wait_send()

    for copy in started:
        copy.wait_send()


def exchange(vectors, active):
    rows, width = vectors.shape
    hbm = pl.BlockSpec(memory_space=pltpu.HBM)
    return pl.pallas_call(
        exchange_kernel,
        out_shape=(
            jax.ShapeDtypeStruct((2, 4, 4, 2, 8, 256), F32),
            jax.ShapeDtypeStruct((2, 16, 2, 8, 128), F32),
            jax.ShapeDtypeStruct((4, rows, width), BF16),
            jax.ShapeDtypeStruct((8, 512), F32),
        ),
        in_specs=[hbm, hbm],
        out_specs=(VMEM, VMEM, VMEM, VMEM),
        scratch_shapes=[
            pltpu.SMEM((8,), jnp.int32),
            pltpu.VMEM((2, rows // 2, width), BF16), pltpu.VMEM((4, rows // 4, width), BF16),
            pltpu.VMEM((256, 256), F32), pltpu.VMEM((128, 256), F32), pltpu.VMEM((3, 32, 256), F32),
            pltpu.VMEM((3, 8, 256), F32), pltpu.VMEM((4, 8, 256), F32),
            pltpu.VMEM((128, 256), F32), pltpu.VMEM((32, 256), F32), pltpu.VMEM((8, 256), F32),
            pltpu.VMEM((256, 256), F32), pltpu.VMEM((128, 256), F32), pltpu.VMEM((16, 2, 8, 128), F32),
            pltpu.VMEM((64, 8, 128), F32), pltpu.VMEM((256, 256), F32),
            pltpu.SemaphoreType.DMA((3,)), pltpu.SemaphoreType.DMA((SEMS,)), pltpu.SemaphoreType.DMA((SEMS,)),
        ],
        compiler_params=pltpu.CompilerParams(
            collective_id=0, has_side_effects=True, vmem_limit_bytes=24 * 2**20
        ),
        name="exchange",
    )(*[pltpu.with_memory_space_constraint(v, pltpu.HBM) for v in (vectors, active)])


def split(value):
    high = value.astype(BF16)
    return high, (value - high.astype(F32)).astype(BF16)


def product(left, right):
    (lh, ll), (rh, rl) = left, right
    dot = functools.partial(jnp.dot, preferred_element_type=F32)
    return dot(lh, rh) + (dot(lh, rl) + dot(ll, rh))


def finish_kernel(
    total_rows, early_ref, late_ref, all_ref, flag_ref, out_ref, matrix, factor, result, out_sem,
):
    s = lax.axis_index("state")
    rows = all_ref.shape[1]
    cols = matrix.shape[0]
    cross = jnp.concatenate([late_ref[:, :, k].reshape(256, 128) for k in (0, 1)], axis=1)
    matrix[0:256, 0:256] = early_ref[:, :, :, 0].reshape(256, 256)
    matrix[256:512, 256:512] = early_ref[:, :, :, 1].reshape(256, 256)
    matrix[0:256, 256:512] = cross
    matrix[256:512, 0:256] = cross.T
    eye = lax.broadcasted_iota(jnp.int32, (cols, cols), 0) == lax.broadcasted_iota(jnp.int32, (cols, cols), 1)
    gram_matrix = matrix[...] + jnp.where(eye & (flag_ref[0:1, :] == 0.0), total_rows, 0.0)
    frob_norm = jnp.sqrt(jnp.sum(gram_matrix * gram_matrix, keepdims=True))
    current = gram_matrix / frob_norm

    panel_eye = lax.broadcasted_iota(jnp.int32, (cols, 128), 0) == lax.broadcasted_iota(jnp.int32, (cols, 128), 1) + s * 128

    def advance(parts, current):
        first = 1.5 * current - 0.5 * product(parts, parts)
        return 1.5 * first - 0.5 * product(split(first), parts)

    matrix[...] = current
    column = matrix[:, pl.ds(pl.multiple_of(s * 128, 128), 128)]
    panel = jnp.where(panel_eye, 1.5, 0.0) - 0.5 * column
    parts = split(current)
    for step in range(2):
        current = advance(parts, current)
        parts = split(current)
        panel = 1.5 * panel - 0.5 * product(parts, split(panel))
    current = advance(parts, current)
    parts = split(current)
    moved = product(parts, split(panel))
    panel = 1.5 * panel - 0.5 * moved
    last = product(parts, split(panel))
    last = 1.5 * last - 0.5 * product(parts, split(last))
    last = 1.5 * last - 0.5 * product(parts, split(last))
    panel = 1.5 * panel - 0.5 * last
    factor[...] = panel * jnp.sqrt(total_rows / frob_norm)

    def factor_of(state):
        return factor[pl.ds(pl.multiple_of(state * 128, 128), 128), :].astype(BF16)

    near = jnp.concatenate([factor_of(0), factor_of(1)], axis=0)
    far = jnp.concatenate([factor_of(2), factor_of(3)], axis=0)
    keep = flag_ref[0:1, pl.ds(pl.multiple_of(s * 128, 128), 128)]
    chunk = 512
    for k in range(rows // chunk):
        block = pl.ds(k * chunk, chunk)
        left = jnp.concatenate([all_ref[0, block], all_ref[1, block]], axis=1)
        right = jnp.concatenate([all_ref[2, block], all_ref[3, block]], axis=1)
        value = jnp.dot(left, near, preferred_element_type=F32) + jnp.dot(right, far, preferred_element_type=F32)
        result[block] = jnp.where(keep == 1.0, value, all_ref[s, block].astype(F32)).astype(BF16)
        pltpu.make_async_copy(result.at[block], out_ref.at[block], out_sem.at[k]).start()
    for k in range(rows // chunk):
        block = pl.ds(k * chunk, chunk)
        pltpu.make_async_copy(result.at[block], out_ref.at[block], out_sem.at[k]).wait()


def finish(total_rows, early, late, everything, flag):
    rows, width = everything.shape[1:]
    return pl.pallas_call(
        functools.partial(finish_kernel, total_rows),
        out_shape=jax.ShapeDtypeStruct((rows, width), BF16),
        in_specs=[VMEM] * 4,
        out_specs=ANY,
        scratch_shapes=[
            pltpu.VMEM((512, 512), F32), pltpu.VMEM((512, 128), F32), pltpu.VMEM((rows, width), BF16),
            pltpu.SemaphoreType.DMA((8,)),
        ],
        compiler_params=pltpu.CompilerParams(vmem_limit_bytes=40 * 2**20),
        name="finish",
    )(early, late, everything, flag)


def shards(vectors, active):
    total_rows = float(vectors.shape[0] * lax.axis_size("row"))
    return finish(total_rows, *exchange(vectors, active))


def solution(mesh):
    in_specs = (P("row", "state"), P())
    out_specs = P("row", "state")
    return jax.shard_map(shards, mesh=mesh, in_specs=in_specs, out_specs=out_specs, check_vma=False)
```

time: 60.6 us -> 52.8 us (0.87)
  Pallas kernels: 57.3 us -> 52.7 us
  local copies, waits for them, and re-layouts: 3.1 us -> 0 us
    pallas_call x1, Pallas kernels: 43.4 us -> 39.8 us  [exchange(): pl.pallas_call(exchange_kernel, out_shape=(jax.ShapeDtypeStruct((2, 4, 4,...]
    unnamed x6 -> x0, local copies, waits for them, and re-layouts: 3.1 us -> none
    pallas_call x1, Pallas kernels: 14 us -> 13 us  [finish(): pl.pallas_call(functools.partial(finish_kernel, total_rows), out_shape=ja...]
where the time goes in v2:
time: 52.8 us; the launch traced here: 52.7 us
  Pallas kernels  52.7 us (100%)
    pallas_call x1, Pallas kernels, exchange(): pl.pallas_call(exchange_kernel, out_shape=(jax.ShapeDtypeStruct((2, 4, 4,...  39.8 us
    pallas_call x1, Pallas kernels, finish(): pl.pallas_call(functools.partial(finish_kernel, total_rows), out_shape=ja...  13 us

profile of v2, /device:TPU:1, one launch (start us, length us, event | category | flops | bytes accessed | tf_op | source)
XLA Modules:
  0.0 52.7 jit_solution(18100147687523789863)
XLA Ops:
  0.0 39.8 %exchange.1 = (f32[2,4,4,2,8,256]{5,4,3,2,1,0:T(8,128)S(1)}, f32[2,16,2,8,128]{4,3,2,1,0:T(8,128)S(1)}, bf16[4,4096,128]{2,1,0:T(8,128)(2,1)S(1)}, f32[8,512]{1,0:T(8,128)S(1)}) custom-call(bf16[4096,128]{1,0:T(8,128)(2,1)} %vec_ref.1, s32[8]{0:T(128)} %active_hbm.1), custom_call_target="tpu_custom_call" | custom-call | tf_op jit(solution)/shard_map/exchange/pallas_call | solution.py:249
  39.8 13.0 %finish.1 = bf16[4096,128]{1,0:T(8,128)(2,1)} custom-call(f32[2,4,4,2,8,256]{5,4,3,2,1,0:T(8,128)S(1)} %get-tuple-element.9.early_ref, f32[2,16,2,8,128]{4,3,2,1,0:T(8,128)S(1)} %get-tuple-element.10.late_ref, bf16[4,4096,128]{2,1,0:T(8,128)(2,1)S(1)} %get-tuple-element.11.all_ref, f32[8,512]{1,0:T(8,128)S(1)} %get-tuple-element.12.flag_ref), custom_call_target="tpu_custom_call" | custom-call | tf_op jit(solution)/shard_map/finish/pallas_call | solution.py:348

commit v3 on v2

--- a/solution.py
+++ b/solution.py
@@ -280,12 +280,31 @@
 
 def product(left, right):
     (lh, ll), (rh, rl) = left, right
-    dot = functools.partial(jnp.dot, preferred_element_type=F32)
-    return dot(lh, rh) + (dot(lh, rl) + dot(ll, rh))
+    return jnp.dot(
+        jnp.concatenate([ll, lh, lh], axis=1), jnp.concatenate([rh, rl, rh], axis=0), preferred_element_type=F32
+    )
+
+
+def mirrored(left, right, below=None):
+    h = left[0].shape[0] // 2
+    upper = [v[:h] for v in left]
+    if below is not None:
+        upper = [jnp.concatenate(pair, axis=0) for pair in zip(upper, below)]
+    top = product(upper, right)
+    low = product([v[h:] for v in left], [v[:, h:] for v in right])
+    top, rest = top[:h], top[h:]
+    return jnp.concatenate([top, jnp.concatenate([top[:, h:].T, low], axis=1)], axis=0), rest
+
+
+def narrow(left, right):
+    (lh, ll), (rh, rl) = left, right
+    rows = lh.shape[0]
+    both = jnp.dot(jnp.concatenate([lh, ll], axis=0), rh, preferred_element_type=F32)
+    return both[:rows] + (both[rows:] + jnp.dot(lh, rl, preferred_element_type=F32))
 
 
 def finish_kernel(
-    total_rows, early_ref, late_ref, all_ref, flag_ref, out_ref, matrix, factor, result, out_sem,
+    total_rows, early_ref, late_ref, all_ref, flag_ref, out_ref, matrix, result, out_sem,
 ):
     s = lax.axis_index("state")
     rows = all_ref.shape[1]
@@ -300,42 +319,34 @@
     frob_norm = jnp.sqrt(jnp.sum(gram_matrix * gram_matrix, keepdims=True))
     current = gram_matrix / frob_norm
 
-    panel_eye = lax.broadcasted_iota(jnp.int32, (cols, 128), 0) == lax.broadcasted_iota(jnp.int32, (cols, 128), 1) + s * 128
-
-    def advance(parts, current):
-        first = 1.5 * current - 0.5 * product(parts, parts)
-        return 1.5 * first - 0.5 * product(split(first), parts)
+    rows_of = pl.ds(pl.multiple_of(s * 128, 128), 128)
+    panel_eye = lax.broadcasted_iota(jnp.int32, (128, cols), 0) + s * 128 == lax.broadcasted_iota(jnp.int32, (128, cols), 1)
+
+    def advance(parts, current, panel):
+        square, moved = mirrored(parts, parts, None if panel is None else split(panel))
+        first = 1.5 * current - 0.5 * square
+        current = 1.5 * first - 0.5 * mirrored(split(first), parts)[0]
+        if panel is not None:
+            panel = 1.5 * panel - 0.5 * moved
+        return split(current), current, panel
 
     matrix[...] = current
-    column = matrix[:, pl.ds(pl.multiple_of(s * 128, 128), 128)]
-    panel = jnp.where(panel_eye, 1.5, 0.0) - 0.5 * column
-    parts = split(current)
-    for step in range(2):
-        current = advance(parts, current)
-        parts = split(current)
-        panel = 1.5 * panel - 0.5 * product(parts, split(panel))
-    current = advance(parts, current)
-    parts = split(current)
-    moved = product(parts, split(panel))
-    panel = 1.5 * panel - 0.5 * moved
-    last = product(parts, split(panel))
-    last = 1.5 * last - 0.5 * product(parts, split(last))
-    last = 1.5 * last - 0.5 * product(parts, split(last))
+    first_panel = jnp.where(panel_eye, 1.5, 0.0) - 0.5 * matrix[rows_of, :]
+    parts, current, _ = advance(split(current), current, None)
+    parts, current, panel = advance(parts, current, first_panel)
+    parts, current, panel = advance(parts, current, panel)
+    panel = 1.5 * panel - 0.5 * narrow(split(panel), parts)
+    last = narrow(split(panel), parts)
+    last = 1.5 * last - 0.5 * narrow(split(last), parts)
+    last = 1.5 * last - 0.5 * narrow(split(last), parts)
     panel = 1.5 * panel - 0.5 * last
-    factor[...] = panel * jnp.sqrt(total_rows / frob_norm)
-
-    def factor_of(state):
-        return factor[pl.ds(pl.multiple_of(state * 128, 128), 128), :].astype(BF16)
-
-    near = jnp.concatenate([factor_of(0), factor_of(1)], axis=0)
-    far = jnp.concatenate([factor_of(2), factor_of(3)], axis=0)
+    factor = (panel * jnp.sqrt(total_rows / frob_norm)).astype(BF16)
     keep = flag_ref[0:1, pl.ds(pl.multiple_of(s * 128, 128), 128)]
     chunk = 512
     for k in range(rows // chunk):
         block = pl.ds(k * chunk, chunk)
-        left = jnp.concatenate([all_ref[0, block], all_ref[1, block]], axis=1)
-        right = jnp.concatenate([all_ref[2, block], all_ref[3, block]], axis=1)
-        value = jnp.dot(left, near, preferred_element_type=F32) + jnp.dot(right, far, preferred_element_type=F32)
+        left = jnp.concatenate([all_ref[k4, block] for k4 in range(4)], axis=1)
+        value = lax.dot_general(left, factor, (((1,), (1,)), ((), ())), preferred_element_type=F32)
         result[block] = jnp.where(keep == 1.0, value, all_ref[s, block].astype(F32)).astype(BF16)
         pltpu.make_async_copy(result.at[block], out_ref.at[block], out_sem.at[k]).start()
     for k in range(rows // chunk):
@@ -351,7 +362,7 @@
         in_specs=[VMEM] * 4,
         out_specs=ANY,
         scratch_shapes=[
-            pltpu.VMEM((512, 512), F32), pltpu.VMEM((512, 128), F32), pltpu.VMEM((rows, width), BF16),
+            pltpu.VMEM((512, 512), F32), pltpu.VMEM((rows, width), BF16),
             pltpu.SemaphoreType.DMA((8,)),
         ],
         compiler_params=pltpu.CompilerParams(vmem_limit_bytes=40 * 2**20),

time: 52.8 us -> 48.2 us (0.913)
  Pallas kernels: 52.7 us -> 48.1 us
    pallas_call x1, Pallas kernels: 13 us -> 8.37 us  [finish(): pl.pallas_call(functools.partial(finish_kernel, total_rows), out_shape=ja...]
where the time goes in v3:
time: 48.2 us; the launch traced here: 48.1 us
  Pallas kernels  48.1 us (100%)
    pallas_call x1, Pallas kernels, exchange(): pl.pallas_call(exchange_kernel, out_shape=(jax.ShapeDtypeStruct((2, 4, 4,...  39.8 us
    pallas_call x1, Pallas kernels, finish(): pl.pallas_call(functools.partial(finish_kernel, total_rows), out_shape=ja...  8.37 us

profile of v3, /device:TPU:1, one launch (start us, length us, event | category | flops | bytes accessed | tf_op | source)
XLA Modules:
  0.0 48.1 jit_solution(1489597785612845601)
XLA Ops:
  0.0 39.8 %exchange.1 = (f32[2,4,4,2,8,256]{5,4,3,2,1,0:T(8,128)S(1)}, f32[2,16,2,8,128]{4,3,2,1,0:T(8,128)S(1)}, bf16[4,4096,128]{2,1,0:T(8,128)(2,1)S(1)}, f32[8,512]{1,0:T(8,128)S(1)}) custom-call(bf16[4096,128]{1,0:T(8,128)(2,1)} %vec_ref.1, s32[8]{0:T(128)} %active_hbm.1), custom_call_target="tpu_custom_call" | custom-call | tf_op jit(solution)/shard_map/exchange/pallas_call | solution.py:249
  39.8 8.4 %finish.1 = bf16[4096,128]{1,0:T(8,128)(2,1)} custom-call(f32[2,4,4,2,8,256]{5,4,3,2,1,0:T(8,128)S(1)} %get-tuple-element.9.early_ref, f32[2,16,2,8,128]{4,3,2,1,0:T(8,128)S(1)} %get-tuple-element.10.late_ref, bf16[4,4096,128]{2,1,0:T(8,128)(2,1)S(1)} %get-tuple-element.11.all_ref, f32[8,512]{1,0:T(8,128)S(1)} %get-tuple-element.12.flag_ref), custom_call_target="tpu_custom_call" | custom-call | tf_op jit(solution)/shard_map/finish/pallas_call | solution.py:359

commit v4 on v3

--- a/solution.py
+++ b/solution.py
@@ -14,8 +14,10 @@
 ANY = pl.BlockSpec(memory_space=pl.ANY)
 VMEM = pl.BlockSpec(memory_space=pltpu.VMEM)
 
-HALF, QUARTER, OWN, LINK, RELAY, CORE, XDIM, YDIM, ZDIM, YBACK, XBACK, CBACK = 0, 1, 5, 6, 10, 14, 15, 18, 21, 24, 27, 30
-LCORE, LOUT, LBACK, LCBACK, SEMS = 31, 32, 33, 34, 35
+HALF, QUARTER, OWN, CORE, XDIM, YDIM, ZDIM, YBACK, XBACK, CBACK = 0, 1, 5, 6, 7, 10, 13, 16, 19, 22
+LCORE, LOUT, LBACK, LCBACK, LINK, RELAY, SEMS = 23, 24, 25, 26, 27, 43, 59
+CHUNKS = 8
+PLAN = ((0,), (1, 2, 3, 4), (5, 6, 7))
 OFFSETS = [(a, b, d) for a in range(4) for b in range(4) for d in range(4)]
 
 
@@ -128,38 +130,43 @@
     arrive(step)
     early_sum3[...] = early_sum2[pl.ds(pl.multiple_of(y * 8, 8), 8), :] + early_y[0] + early_y[1] + early_y[2]
     early_z[z] = early_sum3[...]
-    early_step = start([send(early_sum3, early_z.at[z], ZDIM + d - 1, z_peer(d)) for d in (1, 2, 3)])
+
+    chunk_rows = 2 * quart_rows // CHUNKS
+
+    def chunk_at(chunk, core, frm):
+        part, piece = chunk // (CHUNKS // 2), chunk % (CHUNKS // 2)
+        return all_ref.at[far + part, pl.ds((frm * 2 + core) * quart_rows + piece * chunk_rows, chunk_rows)]
+
+    def link(chunk):
+        part, piece = chunk // (CHUNKS // 2), chunk % (CHUNKS // 2)
+        return [
+            send(
+                quart.at[2 - 2 * to + part, pl.ds(piece * chunk_rows, chunk_rows)],
+                all_ref.at[2 - 2 * to + part, pl.ds(s * quart_rows + piece * chunk_rows, chunk_rows)],
+                LINK + chunk * 2 + to, (to * 2 + c, other_r), recv=LINK + chunk * 2 + zh,
+            )
+            for to in (0, 1)
+        ]
+
+    def relay_copies(chunk, core):
+        blocks = [chunk_at(chunk, core, frm) for frm in (0, 1)]
+        return [send(block, block, RELAY + chunk * 2 + frm, partner) for frm, block in enumerate(blocks)]
+
+    def relay(chunk):
+        for frm in (0, 1):
+            block = chunk_at(chunk, c, frm)
+            send(block, block, LINK + chunk * 2 + frm, partner).wait_recv()
+        start(relay_copies(chunk, c))
 
     for t in range(4):
         send(vec_ref.at[pl.ds(0, quart_rows)], quart.at[t], QUARTER + t, (t, other_r)).wait_recv()
+    early_step = start([send(early_sum3, early_z.at[z], ZDIM + d - 1, z_peer(d)) for d in (1, 2, 3)])
+    for chunk in PLAN[0]:
+        start(link(chunk))
     left = jnp.concatenate([quart[0], quart[1]], axis=1)
     right = jnp.concatenate([quart[2], quart[3]], axis=1)
     late_part[...] = jnp.where(mask[...] == 1.0, gram(left, right), 0.0)
     step = start([send(late_part.at[pl.ds((1 - c) * 128, 128)], late_core, LCORE, partner)])
-
-    def link(part):
-        return [
-            send(
-                quart.at[2 - 2 * to + part],
-                all_ref.at[2 - 2 * to + part, pl.ds(s * quart_rows, quart_rows)],
-                LINK + part * 2 + to,
-                (to * 2 + c, other_r),
-                recv=LINK + part * 2 + zh,
-            )
-            for to in (0, 1)
-        ]
-
-    def relay_copies(part, core):
-        blocks = [all_ref.at[far + part, pl.ds((frm * 2 + core) * quart_rows, quart_rows)] for frm in (0, 1)]
-        return [send(block, block, RELAY + part * 2 + frm, partner) for frm, block in enumerate(blocks)]
-
-    def link_arrive(part):
-        for frm in (0, 1):
-            send(
-                quart.at[0], all_ref.at[far + part, pl.ds((frm * 2 + c) * quart_rows, quart_rows)],
-                LINK + part * 2 + frm, partner,
-            ).wait_recv()
-
     arrive(step)
     total = late_part[pl.ds(pl.multiple_of(c * 128, 128), 128), :] + late_core[...]
     for k in (0, 1):
@@ -181,14 +188,16 @@
             pl.when(odd == 1)(functools.partial(scatter, offset))
         else:
             scatter(offset)
-    start(link(0))
+    for chunk in PLAN[1]:
+        start(link(chunk))
     arrive(early_step)
     early_ref[c, x, y, 0] = early_z[0] + early_z[1]
     early_ref[c, x, y, 1] = early_z[2] + early_z[3]
     early_step = start([
         send(early_ref.at[c, x, y], early_ref.at[c, x, y], YBACK + d - 1, y_peer(d)) for d in (1, 2, 3)
     ])
-    arrive(early_step)
+    for chunk in PLAN[0]:
+        relay(chunk)
 
     here = (c, x * 4 + y, z // 2)
 
@@ -201,10 +210,12 @@
         for offset in sorted(OFFSETS[1:], key=hops, reverse=True):
             send(late_ref.at[here], late_ref.at[here], LBACK, device(offset)).start()
 
+    arrive(early_step)
     early_step = start([send(early_ref.at[c, x], early_ref.at[c, x], XBACK + d - 1, x_peer(d)) for d in (1, 2, 3)])
-    start(link(1))
-    link_arrive(0)
-    start(relay_copies(0, c))
+    for chunk in PLAN[2]:
+        start(link(chunk))
+    for chunk in PLAN[1]:
+        relay(chunk)
     arrive(early_step)
     early_step = start([send(early_ref.at[c], early_ref.at[c], CBACK, partner)])
 
@@ -219,12 +230,12 @@
         send(gathered, gathered, LBACK, partner).wait_recv()
 
     step = start([send(late_ref.at[c], late_ref.at[c], LCBACK, partner)])
-    link_arrive(1)
-    start(relay_copies(1, c))
+    for chunk in PLAN[2]:
+        relay(chunk)
     arrive(early_step)
     arrive(step)
-    arrive(relay_copies(0, 1 - c))
-    arrive(relay_copies(1, 1 - c))
+    for chunk in range(CHUNKS):
+        arrive(relay_copies(chunk, 1 - c))
     send(vec_ref, all_ref.at[near], OWN, partner).wait_recv()
     own.wait()
 

time: 48.2 us -> 46.8 us (0.971)
  Pallas kernels: 48.1 us -> 46.7 us
    pallas_call x1, Pallas kernels: 39.8 us -> 38.3 us  [exchange(): pl.pallas_call(exchange_kernel, out_shape=(jax.ShapeDtypeStruct((2, 4, 4,...]
where the time goes in v4:
time: 46.8 us; the launch traced here: 46.7 us
  Pallas kernels  46.7 us (100%)
    pallas_call x1, Pallas kernels, exchange(): pl.pallas_call(exchange_kernel, out_shape=(jax.ShapeDtypeStruct((2, 4, 4,...  38.3 us
    pallas_call x1, Pallas kernels, finish(): pl.pallas_call(functools.partial(finish_kernel, total_rows), out_shape=ja...  8.38 us

profile of v4, /device:TPU:1, one launch (start us, length us, event | category | flops | bytes accessed | tf_op | source)
XLA Modules:
  0.0 46.7 jit_solution(2045407713913032537)
XLA Ops:
  0.0 38.3 %exchange.1 = (f32[2,4,4,2,8,256]{5,4,3,2,1,0:T(8,128)S(1)}, f32[2,16,2,8,128]{4,3,2,1,0:T(8,128)S(1)}, bf16[4,4096,128]{2,1,0:T(8,128)(2,1)S(1)}, f32[8,512]{1,0:T(8,128)S(1)}) custom-call(bf16[4096,128]{1,0:T(8,128)(2,1)} %vec_ref.1, s32[8]{0:T(128)} %active_hbm.1), custom_call_target="tpu_custom_call" | custom-call | tf_op jit(solution)/shard_map/exchange/pallas_call | solution.py:260
  38.3 8.4 %finish.1 = bf16[4096,128]{1,0:T(8,128)(2,1)} custom-call(f32[2,4,4,2,8,256]{5,4,3,2,1,0:T(8,128)S(1)} %get-tuple-element.9.early_ref, f32[2,16,2,8,128]{4,3,2,1,0:T(8,128)S(1)} %get-tuple-element.10.late_ref, bf16[4,4096,128]{2,1,0:T(8,128)(2,1)S(1)} %get-tuple-element.11.all_ref, f32[8,512]{1,0:T(8,128)S(1)} %get-tuple-element.12.flag_ref), custom_call_target="tpu_custom_call" | custom-call | tf_op jit(solution)/shard_map/finish/pallas_call | solution.py:370

commit v5 on v4

--- a/solution.py
+++ b/solution.py
@@ -14,9 +14,10 @@
 ANY = pl.BlockSpec(memory_space=pl.ANY)
 VMEM = pl.BlockSpec(memory_space=pltpu.VMEM)
 
-HALF, QUARTER, OWN, CORE, XDIM, YDIM, ZDIM, YBACK, XBACK, CBACK = 0, 1, 5, 6, 7, 10, 13, 16, 19, 22
-LCORE, LOUT, LBACK, LCBACK, LINK, RELAY, SEMS = 23, 24, 25, 26, 27, 43, 59
+HALF, OWN, CORE, PLANE, PBACK, ZDIM, CBACK, LCORE, LOUT, LBACK, LCBACK = 0, 1, 2, 3, 4, 5, 8, 9, 10, 11, 12
+LINK, RELAY, QUARTER, SEMS = 13, 29, 45, 61
 CHUNKS = 8
+FIRST = 8
 PLAN = ((0,), (1, 2, 3, 4), (5, 6, 7))
 OFFSETS = [(a, b, d) for a in range(4) for b in range(4) for d in range(4)]
 
@@ -31,8 +32,8 @@
 
 def exchange_kernel(
     vec_ref, active_hbm, early_ref, late_ref, all_ref, flag_ref,
-    active, half, quart, early_part, early_core, early_x, early_y, early_z, early_sum1, early_sum2, early_sum3,
-    late_part, late_core, late_sum, late_got, mask, local_sem, send_sem, recv_sem,
+    active, quart, early_got, early_z, early_sum, early_own,
+    late_part, late_core, late_sum, late_got, mask, local_sem, send_sem, recv_sem, ready,
 ):
     s, r = lax.axis_index("state"), lax.axis_index("row")
     zh, c = s // 2, s % 2
@@ -43,11 +44,18 @@
     partner = (near, r)
     far = 2 - 2 * zh
     rows = vec_ref.shape[0]
-    half_rows, quart_rows = rows // 2, rows // 4
+    quart_rows = rows // 4
+
+    xs = [lax.rem(x + a, 4) * 4 for a in range(4)]
+    ys = [lax.rem(y + b, 4) for b in range(4)]
+    zs = [lax.rem(z + d, 4) for d in range(4)]
+    states = [lax.div(to, 2) * 2 + c for to in zs]
+    lows = [lax.rem(to, 2) * 16 for to in zs]
+    spots = [[to_x + to_y for to_y in ys] for to_x in xs]
 
     def device(offset):
-        to_x, to_y, to_z = [(at + step) % 4 for at, step in zip((x, y, z), offset)]
-        return ((to_z // 2) * 2 + c, (to_z % 2) * 16 + to_x * 4 + to_y)
+        a, b, d = offset
+        return (states[d], lows[d] + spots[a][b])
 
     def x_peer(d):
         return device((d, 0, 0))
@@ -67,18 +75,17 @@
 
     started = []
 
-    def start(copies):
+    def start(copies, wait=True):
         for copy in copies:
             copy.start()
-        started.extend(copies)
+        if wait:
+            started.extend(copies)
         return copies
 
     def arrive(copies):
         for copy in copies:
             copy.wait_recv()
 
-    mine = pltpu.make_async_copy(vec_ref.at[pl.ds(c * half_rows, half_rows)], half.at[c], local_sem.at[0])
-    mine.start()
     flag_copy = pltpu.make_async_copy(active_hbm, active, local_sem.at[1])
     flag_copy.start()
     own = pltpu.make_async_copy(vec_ref, all_ref.at[s], local_sem.at[2])
@@ -91,11 +98,20 @@
         pl.semaphore_signal(barrier, inc=1, device_id=peer, device_id_type=MESH)
     pl.semaphore_wait(barrier, len(peers))
 
-    halves = start([send(vec_ref.at[pl.ds((1 - c) * half_rows, half_rows)], half.at[c], HALF, partner)])
-    start([
-        send(vec_ref.at[pl.ds(t * quart_rows, quart_rows)], quart.at[s], QUARTER + t, (t, other_r), recv=QUARTER + s)
-        for t in range(4)
-    ])
+    start([send(vec_ref, all_ref.at[s], OWN, partner)])
+    edges = [0, FIRST * quart_rows // 16, quart_rows]
+    pieces = [pl.ds(edges[k], edges[k + 1] - edges[k]) for k in (0, 1)]
+
+    def quarter(piece, t, frm):
+        return send(
+            vec_ref.at[pl.ds(t * quart_rows + edges[piece], edges[piece + 1] - edges[piece])],
+            quart.at[frm, pieces[piece]], QUARTER + piece * 4 + t, (t, other_r), recv=QUARTER + piece * 4 + frm,
+        )
+
+    for piece in (0, 1):
+        start([quarter(piece, t, s) for t in range(4)])
+    for d in (1, 2, 3):
+        pl.semaphore_signal(ready, inc=1, device_id=x_peer(d), device_id_type=MESH)
 
     flag_copy.wait()
 
@@ -109,27 +125,26 @@
     flag_ref[...] = flags(flag_ref.shape, 1, 0)
     block = (256, 256)
     mask[...] = flags(block, 0, 0) * flags(block, 1, 4)
-    early_mask = flags(block, 0, zh * 4) * flags(block, 1, zh * 4)
-
-    mine.wait()
-    arrive(halves)
-    both = jnp.concatenate([half[0], half[1]], axis=1)
-    early_part[...] = jnp.where(early_mask == 1.0, gram(both, both), 0.0)
-    step = start([send(early_part.at[pl.ds((1 - c) * 128, 128)], early_core, CORE, partner)])
-    arrive(step)
-    early_sum1[...] = early_part[pl.ds(pl.multiple_of(c * 128, 128), 128), :] + early_core[...]
-    step = start([
-        send(early_sum1.at[pl.ds(((x + d) % 4) * 32, 32)], early_x.at[d - 1], XDIM + d - 1, x_peer(d)) for d in (1, 2, 3)
-    ])
-    start([send(vec_ref, all_ref.at[s], OWN, partner)])
-    arrive(step)
-    early_sum2[...] = early_sum1[pl.ds(pl.multiple_of(x * 32, 32), 32), :] + early_x[0] + early_x[1] + early_x[2]
-    step = start([
-        send(early_sum2.at[pl.ds(((y + d) % 4) * 8, 8)], early_y.at[d - 1], YDIM + d - 1, y_peer(d)) for d in (1, 2, 3)
-    ])
-    arrive(step)
-    early_sum3[...] = early_sum2[pl.ds(pl.multiple_of(y * 8, 8), 8), :] + early_y[0] + early_y[1] + early_y[2]
-    early_z[z] = early_sum3[...]
+    early_mask = flags((128, 256), 0, s * 2) * flags((128, 256), 1, zh * 4)
+
+    own.wait()
+    send(vec_ref, all_ref.at[near], OWN, partner).wait_recv()
+    both = jnp.concatenate([all_ref[s - c], all_ref[s - c + 1]], axis=1)
+    total = jnp.where(early_mask == 1.0, gram(all_ref[s], both), 0.0)
+    early_sum[...] = total.reshape(16, 8, 256)
+    pl.semaphore_wait(ready, 3)
+    spot = x * 4 + y
+    plane = sorted([(a, b, 0) for a in range(4) for b in range(4) if a or b], key=hops, reverse=True)
+    start([
+        send(early_sum.at[((x + a) % 4) * 4 + (y + b) % 4], early_got.at[spot], PLANE, device((a, b, 0)))
+        for a, b, _ in plane
+    ], False)
+    early_got[spot] = early_sum[spot]
+    fifteen = early_got.at[pl.ds(0, 15)]
+    send(fifteen, fifteen, PLANE, partner).wait_recv()
+    early_own[...] = jnp.sum(early_got[...], axis=0)
+    early_z[z] = early_own[...]
+    early_step = start([send(early_own, early_z.at[z], ZDIM + d - 1, z_peer(d)) for d in (1, 2, 3)])
 
     chunk_rows = 2 * quart_rows // CHUNKS
 
@@ -158,9 +173,8 @@
             send(block, block, LINK + chunk * 2 + frm, partner).wait_recv()
         start(relay_copies(chunk, c))
 
-    for t in range(4):
-        send(vec_ref.at[pl.ds(0, quart_rows)], quart.at[t], QUARTER + t, (t, other_r)).wait_recv()
-    early_step = start([send(early_sum3, early_z.at[z], ZDIM + d - 1, z_peer(d)) for d in (1, 2, 3)])
+    for piece in (0, 1):
+        arrive([quarter(piece, 0, t) for t in range(4)])
     for chunk in PLAN[0]:
         start(link(chunk))
     left = jnp.concatenate([quart[0], quart[1]], axis=1)
@@ -175,12 +189,17 @@
     place = x * 16 + y * 4 + z
     outward = sorted([(a, b, d) for a in range(4) for b in range(4) for d in (0, 2)], key=hops, reverse=True)
 
+    owner_z = [[lax.rem(z + d + even, 4) for even in (odd, 1 - odd)] for d in (0, 2)]
+    owner_state = [[lax.div(to, 2) * 2 + c for to in pair] for pair in owner_z]
+    owner_low = [[lax.rem(to, 2) * 16 for to in pair] for pair in owner_z]
+    owner_half = [[lax.div(to, 2) for to in pair] for pair in owner_z]
+
     def scatter(offset):
         a, b, d = offset
-        d = d + (a + b + odd) % 2
-        to_x, to_y, to_z = (x + a) % 4, (y + b) % 4, (z + d) % 4
+        k, even, spot_to = d // 2, (a + b) % 2, spots[a][b]
         send(
-            late_sum.at[to_x * 4 + to_y, to_z // 2], late_got.at[place], LOUT, device((a, b, d))
+            late_sum.at[spot_to, owner_half[k][even]], late_got.at[place], LOUT,
+            (owner_state[k][even], owner_low[k][even] + spot_to),
         ).start()
 
     for offset in outward:
@@ -191,11 +210,9 @@
     for chunk in PLAN[1]:
         start(link(chunk))
     arrive(early_step)
-    early_ref[c, x, y, 0] = early_z[0] + early_z[1]
-    early_ref[c, x, y, 1] = early_z[2] + early_z[3]
-    early_step = start([
-        send(early_ref.at[c, x, y], early_ref.at[c, x, y], YBACK + d - 1, y_peer(d)) for d in (1, 2, 3)
-    ])
+    early_ref[c, spot, 0] = early_z[0] + early_z[1]
+    early_ref[c, spot, 1] = early_z[2] + early_z[3]
+    start([send(early_ref.at[c, spot], early_ref.at[c, spot], PBACK, device(offset)) for offset in plane], False)
     for chunk in PLAN[0]:
         relay(chunk)
 
@@ -210,13 +227,12 @@
         for offset in sorted(OFFSETS[1:], key=hops, reverse=True):
             send(late_ref.at[here], late_ref.at[here], LBACK, device(offset)).start()
 
-    arrive(early_step)
-    early_step = start([send(early_ref.at[c, x], early_ref.at[c, x], XBACK + d - 1, x_peer(d)) for d in (1, 2, 3)])
     for chunk in PLAN[2]:
         start(link(chunk))
     for chunk in PLAN[1]:
         relay(chunk)
-    arrive(early_step)
+    fifteen = early_ref.at[c, pl.ds(0, 15)]
+    send(fifteen, fifteen, PBACK, partner).wait_recv()
     early_step = start([send(early_ref.at[c], early_ref.at[c], CBACK, partner)])
 
     @pl.when(odd == 0)
@@ -236,8 +252,6 @@
     arrive(step)
     for chunk in range(CHUNKS):
         arrive(relay_copies(chunk, 1 - c))
-    send(vec_ref, all_ref.at[near], OWN, partner).wait_recv()
-    own.wait()
 
     @pl.when(odd == 0)
     def _():
@@ -250,6 +264,9 @@
         out = late_got.at[pl.ds(0, 32)]
         send(out, out, LOUT, partner).wait_send()
 
+    send(fifteen, fifteen, PBACK, partner).wait_send()
+    fifteen = early_got.at[pl.ds(0, 15)]
+    send(fifteen, fifteen, PLANE, partner).wait_send()
     for copy in started:
         copy.wait_send()
 
@@ -260,7 +277,7 @@
     return pl.pallas_call(
         exchange_kernel,
         out_shape=(
-            jax.ShapeDtypeStruct((2, 4, 4, 2, 8, 256), F32),
+            jax.ShapeDtypeStruct((2, 16, 2, 8, 256), F32),
             jax.ShapeDtypeStruct((2, 16, 2, 8, 128), F32),
             jax.ShapeDtypeStruct((4, rows, width), BF16),
             jax.ShapeDtypeStruct((8, 512), F32),
@@ -269,13 +286,12 @@
         out_specs=(VMEM, VMEM, VMEM, VMEM),
         scratch_shapes=[
             pltpu.SMEM((8,), jnp.int32),
-            pltpu.VMEM((2, rows // 2, width), BF16), pltpu.VMEM((4, rows // 4, width), BF16),
-            pltpu.VMEM((256, 256), F32), pltpu.VMEM((128, 256), F32), pltpu.VMEM((3, 32, 256), F32),
-            pltpu.VMEM((3, 8, 256), F32), pltpu.VMEM((4, 8, 256), F32),
-            pltpu.VMEM((128, 256), F32), pltpu.VMEM((32, 256), F32), pltpu.VMEM((8, 256), F32),
+            pltpu.VMEM((4, rows // 4, width), BF16), pltpu.VMEM((16, 8, 256), F32),
+            pltpu.VMEM((4, 8, 256), F32), pltpu.VMEM((16, 8, 256), F32), pltpu.VMEM((8, 256), F32),
             pltpu.VMEM((256, 256), F32), pltpu.VMEM((128, 256), F32), pltpu.VMEM((16, 2, 8, 128), F32),
             pltpu.VMEM((64, 8, 128), F32), pltpu.VMEM((256, 256), F32),
             pltpu.SemaphoreType.DMA((3,)), pltpu.SemaphoreType.DMA((SEMS,)), pltpu.SemaphoreType.DMA((SEMS,)),
+            pltpu.SemaphoreType.REGULAR,
         ],
         compiler_params=pltpu.CompilerParams(
             collective_id=0, has_side_effects=True, vmem_limit_bytes=24 * 2**20
@@ -321,8 +337,8 @@
     rows = all_ref.shape[1]
     cols = matrix.shape[0]
     cross = jnp.concatenate([late_ref[:, :, k].reshape(256, 128) for k in (0, 1)], axis=1)
-    matrix[0:256, 0:256] = early_ref[:, :, :, 0].reshape(256, 256)
-    matrix[256:512, 256:512] = early_ref[:, :, :, 1].reshape(256, 256)
+    matrix[0:256, 0:256] = early_ref[:, :, 0].reshape(256, 256)
+    matrix[256:512, 256:512] = early_ref[:, :, 1].reshape(256, 256)
     matrix[0:256, 256:512] = cross
     matrix[256:512, 0:256] = cross.T
     eye = lax.broadcasted_iota(jnp.int32, (cols, cols), 0) == lax.broadcasted_iota(jnp.int32, (cols, cols), 1)

time: 46.8 us -> 46.2 us (0.987)
  Pallas kernels: 46.7 us -> 46.1 us
    pallas_call x1, Pallas kernels: 38.3 us -> 37.8 us  [exchange(): pl.pallas_call(exchange_kernel, out_shape=(jax.ShapeDtypeStruct((2, 16, 2...]
where the time goes in v5:
time: 46.2 us; the launch traced here: 46.1 us
  Pallas kernels  46.1 us (100%)
    pallas_call x1, Pallas kernels, exchange(): pl.pallas_call(exchange_kernel, out_shape=(jax.ShapeDtypeStruct((2, 16, 2...  37.8 us
    pallas_call x1, Pallas kernels, finish(): pl.pallas_call(functools.partial(finish_kernel, total_rows), out_shape=ja...  8.37 us

profile of v5, /device:TPU:1, one launch (start us, length us, event | category | flops | bytes accessed | tf_op | source)
XLA Modules:
  0.0 46.1 jit_solution(7083545182031178224)
XLA Ops:
  0.0 37.8 %exchange.1 = (f32[2,16,2,8,256]{4,3,2,1,0:T(8,128)S(1)}, f32[2,16,2,8,128]{4,3,2,1,0:T(8,128)S(1)}, bf16[4,4096,128]{2,1,0:T(8,128)(2,1)S(1)}, f32[8,512]{1,0:T(8,128)S(1)}) custom-call(bf16[4096,128]{1,0:T(8,128)(2,1)} %vec_ref.1, s32[8]{0:T(128)} %active_hbm.1), custom_call_target="tpu_custom_call" | custom-call | tf_op jit(solution)/shard_map/exchange/pallas_call | solution.py:277
  37.8 8.4 %finish.1 = bf16[4096,128]{1,0:T(8,128)(2,1)} custom-call(f32[2,16,2,8,256]{4,3,2,1,0:T(8,128)S(1)} %get-tuple-element.9.early_ref, f32[2,16,2,8,128]{4,3,2,1,0:T(8,128)S(1)} %get-tuple-element.10.late_ref, bf16[4,4096,128]{2,1,0:T(8,128)(2,1)S(1)} %get-tuple-element.11.all_ref, f32[8,512]{1,0:T(8,128)S(1)} %get-tuple-element.12.flag_ref), custom_call_target="tpu_custom_call" | custom-call | tf_op jit(solution)/shard_map/finish/pallas_call | solution.py:386

commit v6 on v5

--- a/solution.py
+++ b/solution.py
@@ -18,7 +18,7 @@
 LINK, RELAY, QUARTER, SEMS = 13, 29, 45, 61
 CHUNKS = 8
 FIRST = 8
-PLAN = ((0,), (1, 2, 3, 4), (5, 6, 7))
+PLAN = ((0, 1, 2), (3, 4, 5), (6, 7))
 OFFSETS = [(a, b, d) for a in range(4) for b in range(4) for d in range(4)]
 
 
@@ -30,9 +30,32 @@
     return lax.dot_general(left, right, (((0,), (0,)), ((), ())), preferred_element_type=F32)
 
 
+def split(value):
+    high = value.astype(BF16)
+    return high, (value - high.astype(F32)).astype(BF16)
+
+
+def product(left, right):
+    (lh, ll), (rh, rl) = left, right
+    return jnp.dot(
+        jnp.concatenate([ll, lh, lh], axis=1), jnp.concatenate([rh, rl, rh], axis=0), preferred_element_type=F32
+    )
+
+
+def mirrored(left, right, below=None):
+    h = left[0].shape[0] // 2
+    upper = [v[:h] for v in left]
+    if below is not None:
+        upper = [jnp.concatenate(pair, axis=0) for pair in zip(upper, below)]
+    top = product(upper, right)
+    low = product([v[h:] for v in left], [v[:, h:] for v in right])
+    top, rest = top[:h], top[h:]
+    return jnp.concatenate([top, jnp.concatenate([top[:, h:].T, low], axis=1)], axis=0), rest
+
+
 def exchange_kernel(
-    vec_ref, active_hbm, early_ref, late_ref, all_ref, flag_ref,
-    active, quart, early_got, early_z, early_sum, early_own,
+    total_rows, vec_ref, active_hbm, blocks_ref, parts_ref, squares_ref, scale_ref, late_ref, all_ref, flag_ref,
+    early_ref, active, quart, early_got, early_z, early_sum, early_own,
     late_part, late_core, late_sum, late_got, mask, local_sem, send_sem, recv_sem, ready,
 ):
     s, r = lax.axis_index("state"), lax.axis_index("row")
@@ -235,6 +258,22 @@
     send(fifteen, fifteen, PBACK, partner).wait_recv()
     early_step = start([send(early_ref.at[c], early_ref.at[c], CBACK, partner)])
 
+    arrive(early_step)
+    diagonal = lax.broadcasted_iota(jnp.int32, (256, 256), 0) == lax.broadcasted_iota(jnp.int32, (256, 256), 1)
+    values = []
+    for k in (0, 1):
+        idle = diagonal & (flag_ref[0:1, k * 256:k * 256 + 256] == 0.0)
+        values.append(early_ref[:, :, k].reshape(256, 256) + jnp.where(idle, total_rows, 0.0))
+    largest = jnp.maximum(*[jnp.max(value, keepdims=True) for value in values])
+    scale_ref[...] = jnp.broadcast_to(1.0 / largest, scale_ref.shape)
+    for k in (0, 1):
+        value = values[k] * scale_ref[0:1, 0:1]
+        high, low = split(value)
+        blocks_ref[k] = value
+        parts_ref[0, k] = high
+        parts_ref[1, k] = low
+        squares_ref[k] = product((high, low), (high, low))
+
     @pl.when(odd == 0)
     def _():
         gathered = late_got.at[pl.ds(0, 31)]
@@ -248,7 +287,6 @@
     step = start([send(late_ref.at[c], late_ref.at[c], LCBACK, partner)])
     for chunk in PLAN[2]:
         relay(chunk)
-    arrive(early_step)
     arrive(step)
     for chunk in range(CHUNKS):
         arrive(relay_copies(chunk, 1 - c))
@@ -271,20 +309,24 @@
         copy.wait_send()
 
 
-def exchange(vectors, active):
+def exchange(total_rows, vectors, active):
     rows, width = vectors.shape
     hbm = pl.BlockSpec(memory_space=pltpu.HBM)
     return pl.pallas_call(
-        exchange_kernel,
+        functools.partial(exchange_kernel, total_rows),
         out_shape=(
-            jax.ShapeDtypeStruct((2, 16, 2, 8, 256), F32),
+            jax.ShapeDtypeStruct((2, 256, 256), F32),
+            jax.ShapeDtypeStruct((2, 2, 256, 256), BF16),
+            jax.ShapeDtypeStruct((2, 256, 256), F32),
+            jax.ShapeDtypeStruct((8, 128), F32),
             jax.ShapeDtypeStruct((2, 16, 2, 8, 128), F32),
             jax.ShapeDtypeStruct((4, rows, width), BF16),
             jax.ShapeDtypeStruct((8, 512), F32),
         ),
         in_specs=[hbm, hbm],
-        out_specs=(VMEM, VMEM, VMEM, VMEM),
+        out_specs=(VMEM,) * 7,
         scratch_shapes=[
+            pltpu.VMEM((2, 16, 2, 8, 256), F32),
             pltpu.SMEM((8,), jnp.int32),
             pltpu.VMEM((4, rows // 4, width), BF16), pltpu.VMEM((16, 8, 256), F32),
             pltpu.VMEM((4, 8, 256), F32), pltpu.VMEM((16, 8, 256), F32), pltpu.VMEM((8, 256), F32),
@@ -300,29 +342,6 @@
     )(*[pltpu.with_memory_space_constraint(v, pltpu.HBM) for v in (vectors, active)])
 
 
-def split(value):
-    high = value.astype(BF16)
-    return high, (value - high.astype(F32)).astype(BF16)
-
-
-def product(left, right):
-    (lh, ll), (rh, rl) = left, right
-    return jnp.dot(
-        jnp.concatenate([ll, lh, lh], axis=1), jnp.concatenate([rh, rl, rh], axis=0), preferred_element_type=F32
-    )
-
-
-def mirrored(left, right, below=None):
-    h = left[0].shape[0] // 2
-    upper = [v[:h] for v in left]
-    if below is not None:
-        upper = [jnp.concatenate(pair, axis=0) for pair in zip(upper, below)]
-    top = product(upper, right)
-    low = product([v[h:] for v in left], [v[:, h:] for v in right])
-    top, rest = top[:h], top[h:]
-    return jnp.concatenate([top, jnp.concatenate([top[:, h:].T, low], axis=1)], axis=0), rest
-
-
 def narrow(left, right):
     (lh, ll), (rh, rl) = left, right
     rows = lh.shape[0]
@@ -331,26 +350,40 @@
 
 
 def finish_kernel(
-    total_rows, early_ref, late_ref, all_ref, flag_ref, out_ref, matrix, result, out_sem,
+    total_rows, blocks_ref, parts_ref, squares_ref, scale_ref, late_ref, all_ref, flag_ref, out_ref, matrix, result, out_sem,
 ):
     s = lax.axis_index("state")
     rows = all_ref.shape[1]
     cols = matrix.shape[0]
-    cross = jnp.concatenate([late_ref[:, :, k].reshape(256, 128) for k in (0, 1)], axis=1)
-    matrix[0:256, 0:256] = early_ref[:, :, 0].reshape(256, 256)
-    matrix[256:512, 256:512] = early_ref[:, :, 1].reshape(256, 256)
-    matrix[0:256, 256:512] = cross
-    matrix[256:512, 0:256] = cross.T
-    eye = lax.broadcasted_iota(jnp.int32, (cols, cols), 0) == lax.broadcasted_iota(jnp.int32, (cols, cols), 1)
-    gram_matrix = matrix[...] + jnp.where(eye & (flag_ref[0:1, :] == 0.0), total_rows, 0.0)
-    frob_norm = jnp.sqrt(jnp.sum(gram_matrix * gram_matrix, keepdims=True))
-    current = gram_matrix / frob_norm
-
+    scale = scale_ref[0:1, 0:1]
+    cross = jnp.concatenate([late_ref[:, :, k].reshape(256, 128) for k in (0, 1)], axis=1) * scale
+    turned = cross.T
+    one, two = blocks_ref[0], blocks_ref[1]
+    frob_norm = jnp.sqrt(
+        jnp.sum(one * one, keepdims=True) + jnp.sum(two * two, keepdims=True) + 2.0 * jnp.sum(cross * cross, keepdims=True)
+    )
+    inverse_norm = 1.0 / frob_norm
+    cross_parts, turned_parts = split(cross), split(turned)
+    corner = product(
+        [jnp.concatenate([parts_ref[k, 0], cross_parts[k]], axis=1) for k in (0, 1)],
+        [jnp.concatenate([cross_parts[k], parts_ref[k, 1]], axis=0) for k in (0, 1)],
+    )
+    upper = squares_ref[0] + product(cross_parts, turned_parts)
+    lower = squares_ref[1] + product(turned_parts, cross_parts)
+
+    def whole(first, second, third, fourth):
+        return jnp.concatenate(
+            [jnp.concatenate([first, second], axis=1), jnp.concatenate([third, fourth], axis=1)], axis=0
+        )
+
+    current = whole(one, cross, turned, two) * inverse_norm
+    square = whole(upper, corner, corner.T, lower) * inverse_norm * inverse_norm
     rows_of = pl.ds(pl.multiple_of(s * 128, 128), 128)
     panel_eye = lax.broadcasted_iota(jnp.int32, (128, cols), 0) + s * 128 == lax.broadcasted_iota(jnp.int32, (128, cols), 1)
 
-    def advance(parts, current, panel):
-        square, moved = mirrored(parts, parts, None if panel is None else split(panel))
+    def advance(parts, current, panel, square=None):
+        if square is None:
+            square, moved = mirrored(parts, parts, split(panel))
         first = 1.5 * current - 0.5 * square
         current = 1.5 * first - 0.5 * mirrored(split(first), parts)[0]
         if panel is not None:
@@ -359,7 +392,7 @@
 
     matrix[...] = current
     first_panel = jnp.where(panel_eye, 1.5, 0.0) - 0.5 * matrix[rows_of, :]
-    parts, current, _ = advance(split(current), current, None)
+    parts, current, _ = advance(split(current), current, None, square)
     parts, current, panel = advance(parts, current, first_panel)
     parts, current, panel = advance(parts, current, panel)
     panel = 1.5 * panel - 0.5 * narrow(split(panel), parts)
@@ -367,7 +400,7 @@
     last = 1.5 * last - 0.5 * narrow(split(last), parts)
     last = 1.5 * last - 0.5 * narrow(split(last), parts)
     panel = 1.5 * panel - 0.5 * last
-    factor = (panel * jnp.sqrt(total_rows / frob_norm)).astype(BF16)
+    factor = (panel * jnp.sqrt(total_rows * scale / frob_norm)).astype(BF16)
     keep = flag_ref[0:1, pl.ds(pl.multiple_of(s * 128, 128), 128)]
     chunk = 512
     for k in range(rows // chunk):
@@ -381,12 +414,12 @@
         pltpu.make_async_copy(result.at[block], out_ref.at[block], out_sem.at[k]).wait()
 
 
-def finish(total_rows, early, late, everything, flag):
+def finish(total_rows, blocks, parts, squares, scale, late, everything, flag):
     rows, width = everything.shape[1:]
     return pl.pallas_call(
         functools.partial(finish_kernel, total_rows),
         out_shape=jax.ShapeDtypeStruct((rows, width), BF16),
-        in_specs=[VMEM] * 4,
+        in_specs=[VMEM] * 7,
         out_specs=ANY,
         scratch_shapes=[
             pltpu.VMEM((512, 512), F32), pltpu.VMEM((rows, width), BF16),
@@ -394,12 +427,12 @@
         ],
         compiler_params=pltpu.CompilerParams(vmem_limit_bytes=40 * 2**20),
         name="finish",
-    )(early, late, everything, flag)
+    )(blocks, parts, squares, scale, late, everything, flag)
 
 
 def shards(vectors, active):
     total_rows = float(vectors.shape[0] * lax.axis_size("row"))
-    return finish(total_rows, *exchange(vectors, active))
+    return finish(total_rows, *exchange(total_rows, vectors, active))
 
 
 def solution(mesh):

time: 46.2 us -> 45.5 us (0.985)
  Pallas kernels: 46.1 us -> 45.4 us
    pallas_call x1, Pallas kernels: 8.37 us -> 7.8 us  [finish(): pl.pallas_call(functools.partial(finish_kernel, total_rows), out_shape=ja...]
where the time goes in v6:
time: 45.5 us; the launch traced here: 45.4 us
  Pallas kernels  45.4 us (100%)
    pallas_call x1, Pallas kernels, exchange(): pl.pallas_call(functools.partial(exchange_kernel, total_rows), out_shape=...  37.6 us
    pallas_call x1, Pallas kernels, finish(): pl.pallas_call(functools.partial(finish_kernel, total_rows), out_shape=ja...  7.8 us

profile of v6, /device:TPU:1, one launch (start us, length us, event | category | flops | bytes accessed | tf_op | source)
XLA Modules:
  0.0 45.4 jit_solution(14644426004228499591)
XLA Ops:
  0.0 37.6 %exchange.1 = (f32[2,256,256]{2,1,0:T(8,128)S(1)}, bf16[2,2,256,256]{3,2,1,0:T(8,128)(2,1)S(1)}, f32[2,256,256]{2,1,0:T(8,128)S(1)}, f32[8,128]{1,0:T(8,128)S(1)...) custom-call(bf16[4096,128]{1,0:T(8,128)(2,1)} %vec_ref.1, s32[8]{0:T(128)} %active_hbm.1), custom_call_target="tpu_custom_call" | custom-call | tf_op jit(solution)/shard_map/exchange/pallas_call | solution.py:315
  37.6 7.8 %finish.1 = bf16[4096,128]{1,0:T(8,128)(2,1)} custom-call(f32[2,256,256]{2,1,0:T(8,128)S(1)} %get-tuple-element.12.blocks_ref, bf16[2,2,256,256]{3,2,1,0:T(8,128)(2,1)S(1)} %get-tuple-element.13.parts_ref, f32[2,256,256]{2,1,0:T(8,128)S(1)} %get-tuple-element.14.squares_ref, f32[8,128]{1,0:T(8,128)S(1)} %get-tuple-element.15.scale_ref, ...), custom_call_target="tpu_custom_call" | custom-call | tf_op jit(solution)/shard_map/finish/pallas_call | solution.py:419
